TPU v7x, 32 devices: a whole 2x2x4 slice. The times are simulated.
32 devices in a mesh: seq: 4 (over y, core), wt: 8 (over z, x).
Axes of the slice: x: 2, y: 2, z: 4, core: 2. Of those that a mesh axis runs over, the one named last changes fastest.
Arguments:
- tokens: bfloat16 [8, 1024, 512], P('wt', 'seq'), may hold values from -6 to 6
- halted: int32 [8, 1024], P('wt', 'seq'), may hold values 0 or 1
- attn_ids: int32 [8, 1024, 4], P('wt', 'seq'), may hold values from 0 to 11, all different within a row
- ffn_ids: int32 [8, 1024, 2], P('wt', 'seq'), may hold values from 0 to 31, all different within a row; in each aligned block of 256 rows (0 to 255, 256 to 511, ..., all dimensions but the last counted through in order) at most 24 rows name the same one
- norm1: bfloat16 [512], P('wt'), may hold values from 0.25 to 1.75
- attn_router: bfloat16 [512, 12], P('wt'), may hold values from -0.13183594 to 0.13183594
- attn_kv: bfloat16 [512, 1024], P('wt'), may hold values from -0.25 to 0.25
- attn_query: bfloat16 [12, 512, 512], P(None, 'wt'), may hold values from -0.25 to 0.25
- attn_out: bfloat16 [12, 512, 512], P(None, 'wt'), may hold values from -8.4375 to 8.4375
- norm2: bfloat16 [512], P('wt'), may hold values from 0.25 to 1.75
- ffn_router: bfloat16 [512, 32], P('wt'), may hold values from -0.19824219 to 0.19824219
- ffn_in: bfloat16 [32, 512, 2048], P('wt'), may hold values from -0.25 to 0.25
- ffn_out: bfloat16 [32, 2048, 512], P('wt'), may hold values from -0.26367188 to 0.26367188
- halt_weight: bfloat16 [512], P('wt'), may hold values from -0.25 to 0.25
- cotangent: bfloat16 [8, 1024, 512], P('wt', 'seq'), may hold values from -6 to 6
Outputs:
- block_out: bfloat16 [8, 1024, 512], P('wt', 'seq')
- grad_tokens: float32 [8, 1024, 512], P('wt', 'seq')
- grad_norm1: float32 [512], P('wt')
- grad_attn_router: float32 [512, 12], P('wt')
- grad_attn_kv: float32 [512, 1024], P('wt')
- grad_attn_query: float32 [12, 512, 512], P(None, 'wt')
- grad_attn_out: float32 [12, 512, 512], P(None, 'wt')
- grad_norm2: float32 [512], P('wt')
- grad_ffn_router: float32 [512, 32], P('wt')
- grad_ffn_in: float32 [32, 512, 2048], P('wt')
- grad_ffn_out: float32 [32, 2048, 512], P('wt')
- grad_halt: float32 [512], P('wt')
Inputs may be any that keep to these rules, and one draw needn't show every extreme that they name: `attn_ids`: each position names 4 different attention experts. `ffn_ids`: each position names 2 different feed-forward experts; within one sequence's aligned block of 256 positions no expert is named more than 24 times, and some block reaches 24.
All inputs are finite; a program needn't handle non-finite values. No bound on the sum of `halted` on one device may be relied on, other than what follows from the above.
Results may differ from a plain program's by a relative error of at most 0.02.
Values may be sent and summed in bfloat16 or wider, within the bound.
A program may use at most 256 MiB of HBM per device.

v0:
```python
import jax
import jax.numpy as jnp
from jax import lax
from jax.sharding import PartitionSpec as P

HD = 64
EA = 12
EF = 32
KA = 4
BLOCK = 256
CAP = 24


norm_epsilon = 1e-05


def as_sent(array):
    return jax.tree.map(lambda a: a.astype(jnp.bfloat16) if a.dtype == jnp.float32 else a, array)


def layer_norm(stream):
    center = jnp.mean(stream, -1, keepdims=True)
    shifted = stream - center
    spread = lax.rsqrt(jnp.mean(shifted * shifted, -1, keepdims=True) + norm_epsilon)
    return (shifted * spread, spread)


def norm_back(grad_normed, normed, spread, gain):
    scaled = grad_normed * gain
    return spread * (
        scaled
        - jnp.mean(scaled, -1, keepdims=True)
        - normed * jnp.mean(scaled * normed, -1, keepdims=True)
    )


def pick_gates(logits, onehot):
    picked = jnp.sum(onehot * logits[:, :, None, :], -1)
    return jax.nn.softmax(picked, -1)


def gate_back(gates, grad_gates, onehot):
    grad_picked = gates * (grad_gates - jnp.sum(gates * grad_gates, -1, keepdims=True))
    return jnp.sum(onehot * grad_picked[..., None], -2)


def slot_positions(expert_ids):
    seq_count = expert_ids.shape[0]
    flattened = expert_ids.reshape(seq_count, -1)
    member = (flattened[:, :, None] == jnp.arange(EF, dtype=jnp.int32)).astype(jnp.int32)
    earlier = jnp.cumsum(member, 1) - member
    return (flattened * CAP + jnp.sum(earlier * member, -1)).reshape(expert_ids.shape)


def take_rows(table, places):
    picked = jax.vmap(lambda rows_all, where_rows: rows_all[where_rows])(
        table, places.reshape(places.shape[0], -1)
    )
    return picked.reshape(places.shape + (table.shape[-1],))


def attend_forward(query_heads, pair_heads):
    length, head_count = (query_heads.shape[0], query_heads.shape[1])
    queries = query_heads.reshape(length, head_count, KA, HD)
    key_rows = pair_heads[:, :, :HD]
    value_rows = pair_heads[:, :, HD:]
    mixtures = []
    totals = []
    for block_index in range(length // BLOCK):
        start = block_index * BLOCK
        seen = start + BLOCK
        query_block = queries[start:seen]
        scores = jnp.einsum(
            "bhkd,jhd->hbkj", query_block, key_rows[:seen], preferred_element_type=jnp.float32
        ) * HD ** (-0.5)
        highest = jnp.max(scores, -1, keepdims=True)
        log_total = highest + jnp.log(jnp.sum(jnp.exp(scores - highest), -1, keepdims=True))
        weights_low = jnp.exp(scores - log_total).astype(jnp.bfloat16)
        mixture = jnp.einsum(
            "hbkj,jhd->bhkd", weights_low, value_rows[:seen], preferred_element_type=jnp.float32
        )
        mixtures.append(mixture.astype(jnp.bfloat16))
        totals.append(log_total[..., 0])
    return (jnp.concatenate(mixtures, 0).reshape(length, head_count, KA * HD), jnp.stack(totals, 0))


def attend_backward(query_heads, pair_heads, log_total, grad_heads):
    length, head_count = (query_heads.shape[0], query_heads.shape[1])
    queries = query_heads.reshape(length, head_count, KA, HD)
    grad_mix = grad_heads.reshape(length, head_count, KA, HD)
    key_rows = pair_heads[:, :, :HD]
    value_rows = pair_heads[:, :, HD:]
    grad_keys = jnp.zeros((length, head_count, HD), jnp.float32)
    grad_values = jnp.zeros((length, head_count, HD), jnp.float32)
    grad_query_blocks = []
    for block_index in range(length // BLOCK):
        start = block_index * BLOCK
        seen = start + BLOCK
        query_block = queries[start:seen]
        grad_block = grad_mix[start:seen]
        scores = jnp.einsum(
            "bhkd,jhd->hbkj", query_block, key_rows[:seen], preferred_element_type=jnp.float32
        ) * HD ** (-0.5)
        probs_full = jnp.exp(scores - log_total[block_index][..., None])
        grad_probs = jnp.einsum(
            "bhkd,jhd->hbkj", grad_block, value_rows[:seen], preferred_element_type=jnp.float32
        )
        grad_scores = probs_full * (
            grad_probs - jnp.sum(probs_full * grad_probs, -1, keepdims=True)
        )
        grad_scores = grad_scores.astype(jnp.bfloat16)
        grad_query = jnp.einsum(
            "hbkj,jhd->bhkd", grad_scores, key_rows[:seen], preferred_element_type=jnp.float32
        ) * HD ** (-0.5)
        grad_keys = grad_keys.at[:seen].add(
            jnp.einsum(
                "hbkj,bhkd->jhd", grad_scores, query_block, preferred_element_type=jnp.float32
            )
            * HD ** (-0.5)
        )
        grad_values = grad_values.at[:seen].add(
            jnp.einsum(
                "hbkj,bhkd->jhd",
                probs_full.astype(jnp.bfloat16),
                grad_block,
                preferred_element_type=jnp.float32,
            )
        )
        grad_query_blocks.append(grad_query.astype(jnp.bfloat16))
    grad_pairs = jnp.concatenate([grad_keys, grad_values], -1).astype(jnp.bfloat16)
    grad_query_all = jnp.concatenate(grad_query_blocks, 0)
    return (grad_query_all.reshape(length, head_count, KA * HD), grad_pairs)


def attend_items(exchanged):
    query_heads, pair_heads = exchanged
    results = lax.map(
        lambda pieces: attend_forward(pieces[0], pieces[1]), (query_heads, pair_heads)
    )
    return (results[0], results[1], query_heads, pair_heads)


def per_device(
    tokens,
    halted,
    attn_ids,
    ffn_ids,
    norm1,
    attn_router,
    attn_kv,
    attn_query,
    attn_out,
    norm2,
    ffn_router,
    ffn_in,
    ffn_out,
    halt_weight,
    cotangent,
):
    seq_count, local_len, model_width = tokens.shape
    head_count = model_width // HD
    expert_count = ffn_in.shape[0]
    sources = lax.axis_size("wt")
    gain_first, attn_route, key_value, query_gathered, output_gathered = (
        lax.all_gather(norm1, "wt", axis=0, tiled=True),
        lax.all_gather(attn_router, "wt", axis=0, tiled=True),
        lax.all_gather(attn_kv, "wt", axis=0, tiled=True),
        lax.all_gather(attn_query, "wt", axis=1, tiled=True),
        lax.all_gather(attn_out, "wt", axis=1, tiled=True),
    )
    stream_in = tokens.astype(jnp.float32)
    normed_first, spread_first = layer_norm(stream_in)
    attn_input = (normed_first * gain_first.astype(jnp.float32)).astype(jnp.bfloat16)
    attn_logits = jnp.einsum(
        "std,de->ste", attn_input, attn_route, preferred_element_type=jnp.float32
    )
    attn_hot = (attn_ids[..., None] == jnp.arange(EA, dtype=jnp.int32)).astype(jnp.float32)
    hot_low = attn_hot.astype(jnp.bfloat16)
    attn_gates = pick_gates(attn_logits, attn_hot)
    keys_values = jnp.einsum(
        "std,dc->stc", attn_input, key_value, preferred_element_type=jnp.float32
    )
    keys_values = keys_values.astype(jnp.bfloat16).reshape(seq_count, local_len, head_count, 2 * HD)
    query_all = jnp.einsum(
        "std,edc->stec", attn_input, query_gathered, preferred_element_type=jnp.float32
    )
    query_all = query_all.astype(jnp.bfloat16).reshape(seq_count, local_len, EA, head_count, HD)
    queries = jnp.einsum(
        "stke,stehd->sthkd", hot_low, query_all, preferred_element_type=jnp.float32
    )
    queries = queries.astype(jnp.bfloat16).reshape(seq_count, local_len, head_count, KA * HD)
    mix_heads, log_total, query_heads, pair_heads = attend_items(
        (
            lax.all_to_all(queries, "seq", split_axis=2, concat_axis=1, tiled=True),
            lax.all_to_all(keys_values, "seq", split_axis=2, concat_axis=1, tiled=True),
        )
    )
    mix_tokens = lax.all_to_all(
        as_sent(mix_heads), "seq", split_axis=1, concat_axis=2, tiled=True
    ).astype(mix_heads.dtype)
    mix_tokens = mix_tokens.reshape(seq_count, local_len, head_count, KA, HD)
    mix_select = jnp.einsum(
        "stke,sthkd->stehd", hot_low, mix_tokens, preferred_element_type=jnp.float32
    )
    mix_select = mix_select.astype(jnp.bfloat16).reshape(seq_count, local_len, EA, model_width)
    branch = jnp.einsum(
        "stec,ecd->sted", mix_select, output_gathered, preferred_element_type=jnp.float32
    )
    attn_select = jnp.sum(attn_hot * attn_gates[..., None], 2)
    after_attn = stream_in + jnp.sum(attn_select[..., None] * branch, 2)
    gain_second, ffn_route, halting_gathered = (
        lax.all_gather(norm2, "wt", axis=0, tiled=True),
        lax.all_gather(ffn_router, "wt", axis=0, tiled=True),
        lax.all_gather(halt_weight, "wt", axis=0, tiled=True),
    )
    normed_second, spread_second = layer_norm(after_attn)
    ffn_input = (normed_second * gain_second.astype(jnp.float32)).astype(jnp.bfloat16)
    ffn_logits = jnp.einsum("std,de->ste", ffn_input, ffn_route, preferred_element_type=jnp.float32)
    ffn_hot = (ffn_ids[..., None] == jnp.arange(EF, dtype=jnp.int32)).astype(jnp.float32)
    ffn_gates = pick_gates(ffn_logits, ffn_hot)
    places = slot_positions(ffn_ids)
    slot_count = EF * CAP
    place_hot = (places[..., None] == jnp.arange(slot_count, dtype=jnp.int32)).astype(jnp.bfloat16)
    dispatch = jnp.einsum("stkc,std->scd", place_hot, ffn_input, preferred_element_type=jnp.float32)
    dispatch = dispatch.astype(jnp.bfloat16)
    received = lax.all_to_all(dispatch, "wt", split_axis=1, concat_axis=1, tiled=True)
    item_count = received.shape[0]
    arranged_rows = received.reshape(item_count, sources, expert_count, CAP, model_width)
    pre_local = jnp.einsum(
        "swjcd,jdf->swjcf", arranged_rows, ffn_in, preferred_element_type=jnp.float32
    )
    hidden_local = jax.nn.gelu(pre_local, approximate=True).astype(jnp.bfloat16)
    slots_local = jnp.einsum(
        "swjcf,jfd->swjcd", hidden_local, ffn_out, preferred_element_type=jnp.float32
    )
    slots_local = slots_local.astype(jnp.bfloat16).reshape(item_count, -1, model_width)
    returned = lax.all_to_all(slots_local, "wt", split_axis=1, concat_axis=1, tiled=True)
    expert_rows = take_rows(returned, places).astype(jnp.float32)
    after_ffn = after_attn + jnp.sum(ffn_gates[..., None] * expert_rows, 2)
    live = (1 - halted).astype(jnp.float32)[..., None]
    halt = jax.nn.sigmoid(
        jnp.sum(after_ffn * halting_gathered.astype(jnp.float32), -1, keepdims=True)
    )
    keep = live * (1.0 - halt)
    block_out = (stream_in + keep * (after_ffn - stream_in)).astype(jnp.bfloat16)
    gain_second, ffn_route, halting_gathered = (
        lax.all_gather(norm2, "wt", axis=0, tiled=True),
        lax.all_gather(ffn_router, "wt", axis=0, tiled=True),
        lax.all_gather(halt_weight, "wt", axis=0, tiled=True),
    )
    grad_out = cotangent.astype(jnp.float32)
    grad_logit = (
        -live * halt * (1.0 - halt) * jnp.sum((after_ffn - stream_in) * grad_out, -1, keepdims=True)
    )
    grad_halt = jnp.sum(grad_logit * after_ffn, (0, 1))
    grad_after_ffn = keep * grad_out + grad_logit * halting_gathered.astype(jnp.float32)
    grad_stream = grad_out - keep * grad_out
    grad_rows = (ffn_gates[..., None] * grad_after_ffn[:, :, None, :]).astype(jnp.bfloat16)
    grad_ffn_gates = jnp.sum(expert_rows * grad_after_ffn[:, :, None, :], -1)
    grad_slots = jnp.einsum(
        "stkc,stkd->scd", place_hot, grad_rows, preferred_element_type=jnp.float32
    )
    grad_slots = grad_slots.astype(jnp.bfloat16)
    grad_received = lax.all_to_all(grad_slots, "wt", split_axis=1, concat_axis=1, tiled=True)
    grad_received = grad_received.reshape(seq_count, sources, expert_count, CAP, model_width)
    grad_hidden = jnp.einsum(
        "swjcd,jfd->swjcf", grad_received, ffn_out, preferred_element_type=jnp.float32
    )
    grad_ffn_out = jnp.einsum(
        "swjcf,swjcd->jfd", hidden_local, grad_received, preferred_element_type=jnp.float32
    )
    unused_value, gelu_pullback = jax.vjp(
        lambda values: jax.nn.gelu(values, approximate=True), pre_local
    )
    grad_pre = gelu_pullback(grad_hidden)[0].astype(jnp.bfloat16)
    grad_ffn_in = jnp.einsum(
        "swjcd,swjcf->jdf", arranged_rows, grad_pre, preferred_element_type=jnp.float32
    )
    grad_dispatch = jnp.einsum(
        "swjcf,jdf->swjcd", grad_pre, ffn_in, preferred_element_type=jnp.float32
    )
    grad_dispatch = grad_dispatch.astype(jnp.bfloat16).reshape(seq_count, -1, model_width)
    grad_dispatch = lax.all_to_all(grad_dispatch, "wt", split_axis=1, concat_axis=1, tiled=True)
    grad_ffn_logits = gate_back(ffn_gates, grad_ffn_gates, ffn_hot).astype(jnp.bfloat16)
    grad_ffn_router = jnp.einsum(
        "std,ste->de", ffn_input, grad_ffn_logits, preferred_element_type=jnp.float32
    )
    grad_ffn_input = jnp.sum(take_rows(grad_dispatch, places).astype(jnp.float32), 2)
    grad_ffn_input = grad_ffn_input + jnp.einsum(
        "ste,de->std", grad_ffn_logits, ffn_route, preferred_element_type=jnp.float32
    )
    grad_norm2 = jnp.sum(grad_ffn_input * normed_second, (0, 1))
    grad_after_attn = grad_after_ffn + norm_back(
        grad_ffn_input, normed_second, spread_second, gain_second.astype(jnp.float32)
    )
    grad_stream = grad_stream + grad_after_attn
    gain_first, attn_route, key_value, query_gathered, output_gathered = (
        lax.all_gather(norm1, "wt", axis=0, tiled=True),
        lax.all_gather(attn_router, "wt", axis=0, tiled=True),
        lax.all_gather(attn_kv, "wt", axis=0, tiled=True),
        lax.all_gather(attn_query, "wt", axis=1, tiled=True),
        lax.all_gather(attn_out, "wt", axis=1, tiled=True),
    )
    grad_branch = (attn_select[..., None] * grad_after_attn[:, :, None, :]).astype(jnp.bfloat16)
    grad_select = jnp.sum(branch * grad_after_attn[:, :, None, :], -1)
    grad_attn_gates = jnp.sum(attn_hot * grad_select[:, :, None, :], -1)
    grad_attn_out = jnp.einsum(
        "stec,sted->ecd", mix_select, grad_branch, preferred_element_type=jnp.float32
    )
    grad_mix_all = jnp.einsum(
        "sted,ecd->stec", grad_branch, output_gathered, preferred_element_type=jnp.float32
    )
    grad_mix_all = grad_mix_all.reshape(seq_count, local_len, EA, head_count, HD)
    grad_mix = jnp.einsum(
        "stke,stehd->sthkd", attn_hot, grad_mix_all, precision=lax.Precision.HIGHEST
    )
    grad_mix = grad_mix.astype(jnp.bfloat16).reshape(seq_count, local_len, head_count, KA * HD)
    grad_heads = lax.all_to_all(grad_mix, "seq", split_axis=2, concat_axis=1, tiled=True)
    grad_query_heads, grad_pair_heads = lax.map(
        lambda pieces: attend_backward(pieces[0], pieces[1], pieces[2], pieces[3]),
        (query_heads, pair_heads, log_total, grad_heads),
    )
    grad_queries, grad_pairs = (
        lax.all_to_all(
            as_sent(grad_query_heads), "seq", split_axis=1, concat_axis=2, tiled=True
        ).astype(grad_query_heads.dtype),
        lax.all_to_all(grad_pair_heads, "seq", split_axis=1, concat_axis=2, tiled=True),
    )
    grad_queries = grad_queries.reshape(seq_count, local_len, head_count, KA, HD)
    grad_query_all = jnp.einsum(
        "stke,sthkd->stehd", hot_low, grad_queries, preferred_element_type=jnp.float32
    )
    grad_query_all = grad_query_all.astype(jnp.bfloat16).reshape(
        seq_count, local_len, EA, model_width
    )
    grad_pairs = grad_pairs.reshape(seq_count, local_len, 2 * model_width)
    grad_attn_query = jnp.einsum(
        "std,stec->edc", attn_input, grad_query_all, preferred_element_type=jnp.float32
    )
    grad_attn_kv = jnp.einsum(
        "std,stc->dc", attn_input, grad_pairs, preferred_element_type=jnp.float32
    )
    grad_attn_logits = gate_back(attn_gates, grad_attn_gates, attn_hot).astype(jnp.bfloat16)
    grad_attn_router = jnp.einsum(
        "std,ste->de", attn_input, grad_attn_logits, preferred_element_type=jnp.float32
    )
    grad_attn_input = jnp.einsum(
        "stec,edc->std", grad_query_all, query_gathered, preferred_element_type=jnp.float32
    )
    grad_attn_input = grad_attn_input + jnp.einsum(
        "stc,dc->std", grad_pairs, key_value, preferred_element_type=jnp.float32
    )
    grad_attn_input = grad_attn_input + jnp.einsum(
        "ste,de->std", grad_attn_logits, attn_route, preferred_element_type=jnp.float32
    )
    grad_norm1 = jnp.sum(grad_attn_input * normed_first, (0, 1))
    grad_stream = grad_stream + norm_back(
        grad_attn_input, normed_first, spread_first, gain_first.astype(jnp.float32)
    )
    shards = (
        lax.psum_scatter(
            grad_norm1.astype(jnp.bfloat16), "wt", scatter_dimension=0, tiled=True
        ).astype(jnp.float32),
        lax.psum_scatter(
            grad_attn_router.astype(jnp.bfloat16), "wt", scatter_dimension=0, tiled=True
        ).astype(jnp.float32),
        lax.psum_scatter(
            grad_attn_kv.astype(jnp.bfloat16), "wt", scatter_dimension=0, tiled=True
        ).astype(jnp.float32),
        lax.psum_scatter(
            grad_attn_query.astype(jnp.bfloat16), "wt", scatter_dimension=1, tiled=True
        ).astype(jnp.float32),
        lax.psum_scatter(
            grad_attn_out.astype(jnp.bfloat16), "wt", scatter_dimension=1, tiled=True
        ).astype(jnp.float32),
        lax.psum_scatter(
            grad_norm2.astype(jnp.bfloat16), "wt", scatter_dimension=0, tiled=True
        ).astype(jnp.float32),
        lax.psum_scatter(
            grad_ffn_router.astype(jnp.bfloat16), "wt", scatter_dimension=0, tiled=True
        ).astype(jnp.float32),
        lax.psum_scatter(
            grad_halt.astype(jnp.bfloat16), "wt", scatter_dimension=0, tiled=True
        ).astype(jnp.float32),
    )
    totals = (
        lax.psum(shards[0].astype(jnp.bfloat16), "seq").astype(jnp.float32),
        lax.psum(shards[1].astype(jnp.bfloat16), "seq").astype(jnp.float32),
        lax.psum(shards[2].astype(jnp.bfloat16), "seq").astype(jnp.float32),
        lax.psum(shards[3].astype(jnp.bfloat16), "seq").astype(jnp.float32),
        lax.psum(shards[4].astype(jnp.bfloat16), "seq").astype(jnp.float32),
        lax.psum(shards[5].astype(jnp.bfloat16), "seq").astype(jnp.float32),
        lax.psum(shards[6].astype(jnp.bfloat16), "seq").astype(jnp.float32),
        lax.psum(shards[7].astype(jnp.bfloat16), "seq").astype(jnp.float32),
        lax.psum(grad_ffn_in.astype(jnp.bfloat16), "seq").astype(jnp.float32),
        lax.psum(grad_ffn_out.astype(jnp.bfloat16), "seq").astype(jnp.float32),
    )
    return (
        block_out,
        grad_stream,
        totals[0],
        totals[1],
        totals[2],
        totals[3],
        totals[4],
        totals[5],
        totals[6],
        totals[8],
        totals[9],
        totals[7],
    )


def solution(mesh):
    placed = (
        P("wt", "seq", None),
        P("wt", "seq"),
        P("wt", "seq", None),
        P("wt", "seq", None),
        P("wt"),
        P("wt", None),
        P("wt", None),
        P(None, "wt", None),
        P(None, "wt", None),
        P("wt"),
        P("wt", None),
        P("wt", None, None),
        P("wt", None, None),
        P("wt"),
        P("wt", "seq", None),
    )
    return jax.shard_map(
        per_device,
        mesh=mesh,
        in_specs=placed,
        out_specs=(
            P("wt", "seq", None),
            P("wt", "seq", None),
            P("wt"),
            P("wt", None),
            P("wt", None),
            P(None, "wt", None),
            P(None, "wt", None),
            P("wt"),
            P("wt", None),
            P("wt", None, None),
            P("wt", None, None),
            P("wt"),
        ),
        check_vma=False,
    )
```

profile of v0, /device:TPU:9, one launch (start us, length us, event | category | flops | bytes accessed | tf_op | source)
XLA Modules:
  0.0 1496.9 jit_solution(8975232393847958748)
XLA Ops:
  13.9 16.4 %all-reduce.9 = (bf16[512]{0:T(512)(128)(2,1)S(1)}, bf16[512]{0:T(512)(128)(2,1)}, bf16[512]{0:T(512)(128)(2,1)}) all-reduce(bf16[512]{0:T(512)(128)(2,1)S(1)} %dynamic-update-slice.28, bf16[512]{0:T(512)(128)(2,1)S(1)} %dynamic-update-slice.29, bf16[512]{0:T(512)(128)(2,1)S(1)} %dynamic-update-slice.30), channel_id=1, replica_groups=mesh['seq'=4,'wt'=8] {'wt'}, use_global_device_ids=true, to_apply=%add.2 | all-reduce | flops 1536 | bytes 6144
  35.6 14.3 all-gather.6.cloned.1.call-done
  57.4 91.9 %all-gather.8.cloned.1.call-done = bf16[12,512,512]{2,1,0:T(8,128)(2,1)} async-done(((bf16[12,64,512]{2,1,0:T(8,128)(2,1)}), bf16[12,512,512]{2,1,0:T(8,128)(2,1)}) %all-gather.8.cloned.1.call-update) | async-done | bytes 6291472 | tf_op jit(solution)/shard_map/all_gather | solution.py:168
  160.2 12.9 copy.261
  185.6 24.1 %all-gather = bf16[8,64,12]{1,2,0:T(8,128)(2,1)S(1)} all-gather(bf16[1,64,12]{1,2,0:T(8,128)(2,1)S(1)} %bitcast.634), channel_id=1, replica_groups=mesh['seq'=4,'wt'=8] {'wt'}, dimensions={0}, use_global_device_ids=true | all-gather | bytes 13824 | tf_op jit(solution)/shard_map/all_gather | solution.py:166
  233.1 10.2 all-to-all-start.2
  248.2 8.8 all-to-all-done.2
  265.9 10.0 convolution_convert_fusion.1
  275.9 9.7 copy.269
  285.6 8.5 fusion.15
  319.5 28.9 %all-gather.1 = bf16[8,64,32]{1,2,0:T(8,128)(2,1)S(1)} all-gather(bf16[1,64,32]{1,2,0:T(8,128)(2,1)} %bitcast.632), channel_id=1, replica_groups=mesh['seq'=4,'wt'=8] {'wt'}, dimensions={0}, use_global_device_ids=true | all-gather | bytes 36864 | tf_op jit(solution)/shard_map/all_gather | solution.py:213
  390.9 10.5 all-to-all-done.4
  435.1 25.2 %all_to_all.110 = bf16[8,2,24576]{2,1,0:T(2,128)(2,1)S(1)} all-to-all(bf16[8,2,24576]{2,1,0:T(2,128)(2,1)} %reshape.1533), channel_id=1, replica_groups=mesh['seq'=4,'wt'=8] {'wt'}, dimensions={0} | all-to-all | bytes 1572864 | tf_op jit(solution)/shard_map/all_to_all | solution.py:264
  465.1 10.6 fusion.33
  505.0 11.9 all-to-all-done.6
  552.8 15.5 %copy.294 = f32[256,12,8,64]{3,1,2,0:T(8,128)} copy(f32[256,12,8,64]{0,3,2,1:T(8,128)} %bitcast.546) | data formatting | bytes 12582912 | tf_op jit(solution)/shard_map/reshape.409
  568.3 11.8 convert_bitcast_fusion.1
  584.2 22.1 %all_to_all.111 = bf16[1,256,8,256]{1,3,0,2:T(8,128)(2,1)S(1)} all-to-all(bf16[1,256,8,256]{1,3,0,2:T(8,128)(2,1)} %bitcast.564), channel_id=1, replica_groups=mesh['seq'=4,'wt'=8] {'seq'}, dimensions={2} | all-to-all | bytes 2097152 | tf_op jit(solution)/shard_map/all_to_all | solution.py:318
  651.9 12.3 all_to_all.112
  684.6 17.2 %all_to_all.113 = bf16[1,1024,2,256]{3,2,0,1:T(2,128)(2,1)S(1)} all-to-all(bf16[1,1024,2,256]{3,2,0,1:T(2,128)(2,1)S(1)} %copy.298), channel_id=1, replica_groups=mesh['seq'=4,'wt'=8] {'seq'}, dimensions={1} | all-to-all | bytes 2097152 | tf_op jit(solution)/shard_map/all_to_all | solution.py:324
  712.8 8.3 copy.302
  725.6 14.3 copy.309
  741.9 9.1 bitcast_convert_fusion
  763.6 89.7 %reduce-scatter.14.cloned.1.call-done = bf16[12,64,512]{2,1,0:T(8,128)(2,1)} async-done(((bf16[12,512,512]{2,1,0:T(8,128)(2,1)}), bf16[12,64,512]{2,1,0:T(8,128)(2,1)}) %reduce-scatter.14.cloned.1.call-update) | async-done | bytes 786448 | tf_op jit(solution)/shard_map/reduce_scatter | solution.py:373
  853.3 152.1 %reduce-scatter.12.cloned.1.call-done = bf16[12,64,512]{2,0,1:T(8,128)(2,1)} async-done(((bf16[12,512,512]{2,0,1:T(8,128)(2,1)}), bf16[12,64,512]{2,0,1:T(8,128)(2,1)}) %reduce-scatter.12.cloned.1.call-update) | async-done | bytes 786448 | tf_op jit(solution)/shard_map/reduce_scatter | solution.py:370
  1006.3 62.4 %reduce-scatter.18.cloned.1.call-done = bf16[64,32]{1,0:T(8,128)(2,1)} async-done(((bf16[512,32]{1,0:T(8,128)(2,1)}), bf16[64,32]{1,0:T(8,128)(2,1)}) %reduce-scatter.18.cloned.1.call-update) | async-done | bytes 4112
  1069.7 62.8 %reduce-scatter.16.cloned.1.call-done = bf16[64,12]{1,0:T(8,128)(2,1)} async-done(((bf16[512,12]{1,0:T(8,128)(2,1)}), bf16[64,12]{1,0:T(8,128)(2,1)}) %reduce-scatter.16.cloned.1.call-update) | async-done | bytes 1552
  1141.1 13.8 all-reduce.8
  1155.2 16.1 %all-reduce.10 = (bf16[64]{0:T(256)(128)(2,1)S(1)}, bf16[64,12]{0,1:T(8,128)(2,1)S(1)}, bf16[64]{0:T(256)(128)(2,1)S(1)}, bf16[64,32]{0,1:T(8,128)(2,1)S(1)}, bf16[64]{0:T(256)(128)(2,1)S(1)}) all-reduce(bf16[64]{0:T(256)(128)(2,1)S(1)} %dynamic-slice.82, bf16[64,12]{0,1:T(8,128)(2,1)S(1)} %copy.341, ...), channel_id=1, replica_groups=mesh['seq'=4,'wt'=8] {'seq'}, use_global_device_ids=true, to_apply=%region_45.46 | all-reduce | flops 3008 | bytes 12032 | tf_op jit(solution)/shard_map/psum | solution.py:387
  1174.0 285.6 %all-reduce.14.cloned.1.call-done = (bf16[64,1024]{1,0:T(8,128)(2,1)}, bf16[12,64,512]{2,0,1:T(8,128)(2,1)}, bf16[12,64,512]{2,1,0:T(8,128)(2,1)}, bf16[4,512,2048]{2,1,0:T(8,128)(2,1)}, bf16[4,2048,512]{2,1,0:T(8,128)(2,1)}) async-done(((bf16[64,1024]{1,0:T(8,128)(2,1)}, bf16[12,64,512]{2,0,1:T(8,128)(2,1)}, bf16[12,64,512]{2,1,0:T(8,128)(2,1)}, bf16[4,512,2048]{2,1,0:T(8,128)(2,1)}, ...) | async-done | bytes 18481168 | tf_op jit(solution)/shard_map/psum | solution.py:389
  1466.6 11.7 convert_element_type.511
  1478.2 11.9 convert_element_type.513
  (452 shorter events, 369.1 us)
Async XLA Ops:
  7.2 42.8 %all-gather.6.cloned.1.call-start = ((), (), s32[]{:S(2)}) async-start(), calls=%async_computation.15 | async-start | bytes 1179648 | tf_op jit(solution)/shard_map/all_gather | solution.py:167
  7.9 141.4 %all-gather.8.cloned.1.call-start = ((), (), s32[]{:S(2)}) async-start(), calls=%async_computation.16 | async-start | bytes 7077888 | tf_op jit(solution)/shard_map/all_gather | solution.py:168
  8.7 276.9 %all-gather.10.cloned.1.call-start = ((), (), s32[]{:S(2)}) async-start(), calls=%async_computation.17 | async-start | bytes 7077888 | tf_op jit(solution)/shard_map/all_gather | solution.py:169
  30.4 125.2 %copy-start.64 = (f32[512]{0:T(512)}, f32[512]{0:T(512)S(1)}, u32[]{:S(2)}) copy-start(f32[512]{0:T(512)S(1)} %convert_element_type.425) | copy-start | bytes 6148
  32.0 180.3 %copy-start.40 = (s32[1,256,2]{2,1,0:T(8,128)}, s32[1,256,2]{2,1,0:T(8,128)S(1)}, u32[]{:S(2)}) copy-start(s32[1,256,2]{2,1,0:T(8,128)S(1)} %copy.271) | copy-start | bytes 6148
  33.3 122.3 %copy-start.71 = (f32[256]{0:T(256)}, f32[256]{0:T(256)S(1)}, u32[]{:S(2)}) copy-start(f32[256]{0:T(256)S(1)} %broadcast_multiply_fusion.6) | copy-start | bytes 3076
  34.5 121.1 %copy-start.86 = (f32[256]{0:T(256)}, f32[256]{0:T(256)S(1)}, u32[]{:S(2)}) copy-start(f32[256]{0:T(256)S(1)} %add_rsqrt_fusion.1) | copy-start | bytes 3076
  35.6 207.8 %copy-start.16 = (bf16[1,256,512]{2,1,0:T(8,128)(2,1)}, bf16[1,256,512]{2,1,0:T(8,128)(2,1)S(1)}, u32[]{:S(2)}) copy-start(bf16[1,256,512]{2,1,0:T(8,128)(2,1)S(1)} %fusion.113) | copy-start | bytes 786436
  52.6 127.8 %all-to-all-start = ((bf16[1,256,8,128]{3,1,0,2:T(8,128)(2,1)}), bf16[1,256,8,128]{3,1,0,2:T(8,128)(2,1)S(1)}, u32[]{:S(2)}, u32[]{:S(2)}) async-start(bf16[1,256,8,128]{3,1,0,2:T(8,128)(2,1)} %copy.258), calls=%async_computation | async-start | bytes 1048576 | tf_op jit(solution)/shard_map/all_to_all | solution.py:195
  180.4 33.3 %all-to-all-start.1 = ((bf16[1,256,8,256]{1,3,0,2:T(8,128)(2,1)}), bf16[1,256,8,256]{1,3,0,2:T(8,128)(2,1)S(1)}, u32[]{:S(2)}, u32[]{:S(2)}) async-start(bf16[1,256,8,256]{1,3,0,2:T(8,128)(2,1)} %bitcast.17), calls=%async_computation.1 | async-start | bytes 2097152 | tf_op jit(solution)/shard_map/all_to_all | solution.py:194
  213.7 406.3 %copy-start.9 = (bf16[1024,2,128]{0,2,1:T(8,128)(2,1)}, bf16[1024,2,128]{0,2,1:T(8,128)(2,1)S(1)}, u32[]{:S(2)}) copy-start(bf16[1024,2,128]{0,2,1:T(8,128)(2,1)S(1)} %squeeze.33) | copy-start | bytes 1572868
  233.1 23.8 %all-to-all-start.2 = ((bf16[1,1024,2,256]{3,2,0,1:T(2,128)(2,1)}), bf16[1,1024,2,256]{3,2,0,1:T(2,128)(2,1)}, u32[]{:S(2)}, u32[]{:S(2)}) async-start(bf16[1,1024,2,256]{3,2,0,1:T(2,128)(2,1)} %copy.265), calls=%async_computation.2 | async-start | bytes 2097152 | tf_op jit(solution)/shard_map/all_to_all | solution.py:198
  245.9 48.6 %copy-start.66 = (f32[512]{0:T(512)}, f32[512]{0:T(512)S(1)}, u32[]{:S(2)}) copy-start(f32[512]{0:T(512)S(1)} %convert_element_type.447) | copy-start | bytes 6148
  294.3 63.7 %copy-start.12 = (f32[1,256,512]{2,1,0:T(8,128)}, f32[1,256,512]{2,1,0:T(8,128)S(1)}, u32[]{:S(2)}) copy-start(f32[1,256,512]{2,1,0:T(8,128)S(1)} %get-tuple-element.296) | copy-start | bytes 1572868
  294.3 63.7 %copy-start.73 = (f32[256]{0:T(256)}, f32[256]{0:T(256)S(1)}, u32[]{:S(2)}) copy-start(f32[256]{0:T(256)S(1)} %broadcast_multiply_fusion.5) | copy-start | bytes 3076
  294.7 95.0 %copy-start.26 = (bf16[256,512]{1,0:T(8,128)(2,1)}, bf16[256,512]{1,0:T(8,128)(2,1)S(1)}, u32[]{:S(2)}) copy-start(bf16[256,512]{1,0:T(8,128)(2,1)S(1)} %fusion.140) | copy-start | bytes 786436
  308.5 43.6 %all-to-all-start.3 = ((bf16[8,2,24576]{2,1,0:T(2,128)(2,1)}), bf16[8,2,24576]{2,1,0:T(2,128)(2,1)}, u32[]{:S(2)}, u32[]{:S(2)}) async-start(bf16[8,2,24576]{2,1,0:T(2,128)(2,1)} %reshape.1529), calls=%async_computation.3 | async-start | bytes 1572864 | tf_op jit(solution)/shard_map/all_to_all | solution.py:226
  382.0 19.4 %all-to-all-start.4 = ((bf16[8,2,24576]{2,1,0:T(2,128)(2,1)}), bf16[8,2,24576]{2,1,0:T(2,128)(2,1)}, u32[]{:S(2)}, u32[]{:S(2)}) async-start(bf16[8,2,24576]{2,1,0:T(2,128)(2,1)} %reshape.1531), calls=%async_computation.4 | async-start | bytes 1572864 | tf_op jit(solution)/shard_map/all_to_all | solution.py:237
  496.1 20.8 %all-to-all-start.6 = ((bf16[8,2,24576]{2,1,0:T(2,128)(2,1)}), bf16[8,2,24576]{2,1,0:T(2,128)(2,1)}, u32[]{:S(2)}, u32[]{:S(2)}) async-start(bf16[8,2,24576]{2,1,0:T(2,128)(2,1)} %reshape.1535), calls=%async_computation.6 | async-start | bytes 1572864 | tf_op jit(solution)/shard_map/all_to_all | solution.py:283
  501.0 262.6 %reduce-scatter.10.cloned.1.call-start = ((), (), s32[]{:S(2)}) async-start(), calls=%async_computation.18 | async-start | bytes 1179648 | tf_op jit(solution)/shard_map/reduce_scatter | solution.py:367
  669.6 183.7 %reduce-scatter.14.cloned.1.call-start = ((), (), s32[]{:S(2)}) async-start(), calls=%async_computation.20 | async-start | bytes 7077888 | tf_op jit(solution)/shard_map/reduce_scatter | solution.py:373
  675.1 330.3 %reduce-scatter.12.cloned.1.call-start = ((), (), s32[]{:S(2)}) async-start(), calls=%async_computation.19 | async-start | bytes 9437184 | tf_op jit(solution)/shard_map/reduce_scatter | solution.py:370
  740.0 328.7 %reduce-scatter.18.cloned.1.call-start = ((), (), s32[]{:S(2)}) async-start(), calls=%async_computation.22 | async-start | bytes 147456
  741.8 390.6 %reduce-scatter.16.cloned.1.call-start = ((), (), s32[]{:S(2)}) async-start(), calls=%async_computation.21 | async-start | bytes 147456
  755.6 704.0 %all-reduce.14.cloned.1.call-start = ((), (), s32[]{:S(2)}) async-start(), calls=%async_computation.23 | async-start | bytes 37486592 | tf_op jit(solution)/shard_map/psum | solution.py:389
  1005.4 64.0 %copy-start.59 = (bf16[512,12]{0,1:T(8,128)(2,1)S(1)}, bf16[512,12]{0,1:T(8,128)(2,1)}, u32[]{:S(2)}) copy-start(bf16[512,12]{0,1:T(8,128)(2,1)} %reshape.1487) | copy-start | bytes 36868
  1005.4 133.5 %copy-start.19 = (bf16[1,256,512]{2,1,0:T(8,128)(2,1)S(1)}, bf16[1,256,512]{2,1,0:T(8,128)(2,1)}, u32[]{:S(2)}) copy-start(bf16[1,256,512]{2,1,0:T(8,128)(2,1)} %param.35) | copy-start | bytes 786436
  1005.4 133.5 %copy-start.24 = (bf16[1,256,4,2,128]{1,4,3,2,0:T(8,128)(2,1)S(1)}, bf16[1,256,4,2,128]{1,4,3,2,0:T(8,128)(2,1)}, u32[]{:S(2)}) copy-start(bf16[1,256,4,2,128]{1,4,3,2,0:T(8,128)(2,1)} %copy.308) | copy-start | bytes 1572868
  1005.4 133.5 %copy-start.25 = (bf16[512,1024]{1,0:T(8,128)(2,1)S(1)}, bf16[512,1024]{1,0:T(8,128)(2,1)}, u32[]{:S(2)}) copy-start(bf16[512,1024]{1,0:T(8,128)(2,1)} %all-gather.6.cloned.1.call-done) | copy-start | bytes 3145732
  1005.5 133.5 %copy-start.65 = (f32[512]{0:T(512)S(1)}, f32[512]{0:T(512)}, u32[]{:S(2)}) copy-start(f32[512]{0:T(512)} %copy-done.64) | copy-start | bytes 6148
  1005.5 133.5 %copy-start.72 = (f32[256]{0:T(256)S(1)}, f32[256]{0:T(256)}, u32[]{:S(2)}) copy-start(f32[256]{0:T(256)} %copy-done.71) | copy-start | bytes 3076
  1005.5 133.5 %copy-start.87 = (f32[256]{0:T(256)S(1)}, f32[256]{0:T(256)}, u32[]{:S(2)}) copy-start(f32[256]{0:T(256)} %copy-done.86) | copy-start | bytes 3076
  (89 other events, 772.3 us)
Sparse Core Ops, SparseCore 0:
  10.1 39.7 all-gather.5
  52.1 97.1 all-gather.7
  151.5 97.8 all-gather.9
  669.7 61.0 reduce-scatter.9
  734.7 118.5 reduce-scatter.13
  857.8 147.5 reduce-scatter.11
  1009.3 59.2 reduce-scatter.17
  1072.5 59.8 reduce-scatter.15
  1136.1 323.4 all-reduce.13
where the time goes:
time: 1510 us; the launch traced here: 1500 us
  waiting for transfers between devices  792 us (52%)
  local copies, waits for them, and re-layouts  197 us (13%)
  blocking collectives  176 us (12%)
  matrix products  173 us (11%)
  other arithmetic  102 us (7%)
  starting transfers between devices  39.8 us (3%)
  between operations  17.2 us (1%)
    psum x1, waiting for transfers between devices, per_device(): lax.psum(shards[2].astype(jnp.bfloat16), 'seq').astype(jnp.float32)  286 us
    reduce_scatter x1, waiting for transfers between devices, per_device(): lax.psum_scatter(grad_attn_query.astype(jnp.bfloat16), 'wt', scatter_dime...  152 us
    unnamed x11, waiting for transfers between devices  127 us
    all_gather x1, waiting for transfers between devices, per_device(): lax.all_gather(attn_query, 'wt', axis=1, tiled=True)  91.9 us
    reduce_scatter x1, waiting for transfers between devices, per_device(): lax.psum_scatter(grad_attn_out.astype(jnp.bfloat16), 'wt', scatter_dimens...  89.7 us
    unnamed x242, local copies, waits for them, and re-layouts  55.8 us
    another operation x10, local copies, waits for them, and re-layouts  35.1 us
    unnamed x2, blocking collectives  30.3 us
  transfers between devices with their start and end apart: 15, of which 10 were waited for; matrix products, arithmetic and copies ran while one was open for 13% of the time, Pallas kernels for 0%

commit v1 on v0

v1 whole, which is shorter than its diff:
```python
import functools

import jax
import jax.numpy as jnp
from jax import lax
from jax.experimental import pallas as pl
from jax.experimental.pallas import tpu as pltpu
from jax.sharding import PartitionSpec as P

HD = 64
EA = 12
EF = 32
KA = 4
KF = 2
CAP = 24
EPS = 1e-05
BF = jnp.bfloat16
F32 = jnp.float32

C_N1, C_N2, C_HALT, C_AR, C_FR, C_END = 0, 1, 2, 3, 15, 47


def dot(a, b, ca=1, cb=0):
    return lax.dot_general(a, b, (((ca,), (cb,)), ((), ())), preferred_element_type=F32)


def layer_norm(stream):
    center = jnp.mean(stream, -1, keepdims=True)
    shifted = stream - center
    spread = lax.rsqrt(jnp.mean(shifted * shifted, -1, keepdims=True) + EPS)
    return shifted * spread, spread


def norm_back(grad_normed, normed, spread, gain):
    scaled = grad_normed * gain
    return spread * (
        scaled
        - jnp.mean(scaled, -1, keepdims=True)
        - normed * jnp.mean(scaled * normed, -1, keepdims=True)
    )


def gelu_parts(v):
    c0, c1 = 0.7978845608028654, 0.044715
    v2 = v * v
    t = jnp.tanh(c0 * (v + c1 * (v2 * v)))
    half = 0.5 * (1.0 + t)
    value = v * half
    slope = half + 0.5 * v * (1.0 - t * t) * (c0 * (1.0 + 3.0 * c1 * v2))
    return value, slope


def vmem():
    return pl.BlockSpec(memory_space=pltpu.VMEM)


def attn_fwd_kernel(
    nb, hd, x_ref, ids_ref, small_ref, wq_ref, wkv_ref, wout_ref,
    part_ref, q_ref, kv_ref, mix_ref, gate_ref,
    kv_scr, qa_scr, a_scr,
):
    T = x_ref.shape[0]
    C = hd * HD
    b = pl.program_id(0)
    xb = x_ref[...]
    ids = ids_ref[...]
    kvb = dot(xb, wkv_ref[...]).astype(BF)
    kv_ref[...] = kvb
    kv_scr[pl.ds(pl.multiple_of(b * T, T), T), :] = kvb
    logits = dot(xb, small_ref[...])
    lane = lax.broadcasted_iota(jnp.int32, logits.shape, 1)
    picked = [
        jnp.sum(jnp.where(lane == ids[:, k : k + 1] + C_AR, logits, 0.0), -1, keepdims=True)
        for k in range(KA)
    ]
    top = functools.reduce(jnp.maximum, picked)
    ex = [jnp.exp(p - top) for p in picked]
    tot = functools.reduce(jnp.add, ex)
    gates = [e / tot for e in ex]
    gate_ref[...] = jnp.concatenate(gates, 1)

    qa_scr[...] = dot(xb, wq_ref[...])
    for k in range(KA):
        idk = jnp.broadcast_to(ids[:, k : k + 1], (T, C))
        acc = jnp.zeros((T, C), F32)
        for e in range(EA):
            acc = jnp.where(idk == e, qa_scr[:, e * C : (e + 1) * C], acc)
        q_ref[k] = (acc * (HD**-0.5)).astype(BF)

    for blk in range(nb):

        @pl.when(b == blk)
        def _(blk=blk):
            seen = (blk + 1) * T
            for i in range(hd):
                keys = kv_scr[0:seen, i * 2 * HD : i * 2 * HD + HD]
                vals = kv_scr[0:seen, i * 2 * HD + HD : (i + 1) * 2 * HD]

                def body(k, carry):
                    qk = q_ref[k, :, i * HD : (i + 1) * HD]
                    s = dot(qk, keys, 1, 1)
                    m = jnp.max(s, -1, keepdims=True)
                    p = jnp.exp(s - m)
                    l = jnp.sum(p, -1, keepdims=True)
                    o = dot(p.astype(BF), vals) / l
                    mix_ref[k, :, i * HD : (i + 1) * HD] = o.astype(BF)
                    return carry

                lax.fori_loop(0, KA, body, 0, unroll=2)

    scatter_pairs(ids, [gates[k] * mix_ref[k].astype(F32) for k in range(KA)], a_scr, C)
    part_ref[...] = dot(a_scr[...], wout_ref[...]).astype(part_ref.dtype)


def scatter_pairs(ids, rows, out_ref, C):
    T = ids.shape[0]
    idk = [jnp.broadcast_to(ids[:, k : k + 1], (T, C)) for k in range(KA)]
    for e in range(EA):
        acc = jnp.zeros((T, C), F32)
        for k in range(KA):
            acc = jnp.where(idk[k] == e, rows[k], acc)
        out_ref[:, e * C : (e + 1) * C] = acc.astype(BF)


def attn_forward(x_all, ids_all, small, wq, wkv, wout, T, hd):
    L, D = x_all.shape
    nb = L // T
    C = hd * HD
    return pl.pallas_call(
        functools.partial(attn_fwd_kernel, nb, hd),
        name="attn_forward",
        grid=(nb,),
        out_shape=(
            jax.ShapeDtypeStruct((L, D), BF),
            jax.ShapeDtypeStruct((KA, L, C), BF),
            jax.ShapeDtypeStruct((L, 2 * C), BF),
            jax.ShapeDtypeStruct((KA, L, C), BF),
            jax.ShapeDtypeStruct((L, KA), F32),
        ),
        in_specs=[
            pl.BlockSpec((T, D), lambda b: (b, 0)),
            pl.BlockSpec((T, KA), lambda b: (b, 0)),
            vmem(), vmem(), vmem(), vmem(),
        ],
        out_specs=(
            pl.BlockSpec((T, D), lambda b: (b, 0)),
            pl.BlockSpec((KA, T, C), lambda b: (0, b, 0)),
            pl.BlockSpec((T, 2 * C), lambda b: (b, 0)),
            pl.BlockSpec((KA, T, C), lambda b: (0, b, 0)),
            pl.BlockSpec((T, KA), lambda b: (b, 0)),
        ),
        scratch_shapes=[
            pltpu.VMEM((L, 2 * C), BF),
            pltpu.VMEM((T, EA * C), F32),
            pltpu.VMEM((T, EA * C), BF),
        ],
    )(x_all, ids_all, small, wq, wkv, wout)


def attn_bwd_kernel(
    nb, hd, x_ref, d_ref, ids_ref, gate_ref, q_ref, kv_ref, mix_ref, wq_ref, wkv_ref, wout_ref,
    dx_ref, dg_ref, gq_ref, gkv_ref, gout_ref,
    gq_scr, gkv_scr, gout_scr, dkv_scr, big_scr, a_scr, do_scr, dq_scr, pt_scr, ds_scr,
):
    T = x_ref.shape[0]
    C = hd * HD
    step = pl.program_id(0)
    b = nb - 1 - step

    @pl.when(step == 0)
    def _():
        gq_scr[...] = jnp.zeros_like(gq_scr)
        gkv_scr[...] = jnp.zeros_like(gkv_scr)
        gout_scr[...] = jnp.zeros_like(gout_scr)
        dkv_scr[...] = jnp.zeros_like(dkv_scr)

    xb = x_ref[...]
    db = d_ref[...]
    ids = ids_ref[...]
    gates = gate_ref[...]
    big_scr[...] = dot(db, wout_ref[...], 1, 1)
    dgs = []
    for k in range(KA):
        idk = jnp.broadcast_to(ids[:, k : k + 1], (T, C))
        acc = jnp.zeros((T, C), F32)
        for e in range(EA):
            acc = jnp.where(idk == e, big_scr[:, e * C : (e + 1) * C], acc)
        dgs.append(jnp.sum(acc * mix_ref[k].astype(F32), -1, keepdims=True))
        do_scr[k] = (acc * gates[:, k : k + 1]).astype(BF)
    dg_ref[...] = jnp.concatenate(dgs, 1)
    scatter_pairs(ids, [gates[:, k : k + 1] * mix_ref[k].astype(F32) for k in range(KA)], a_scr, C)
    gout_scr[...] += dot(a_scr[...], db, 0, 0)

    for blk in range(nb):

        @pl.when(b == blk)
        def _(blk=blk):
            seen = (blk + 1) * T
            for i in range(hd):
                lo, mid, hi = i * 2 * HD, i * 2 * HD + HD, (i + 1) * 2 * HD
                keys = kv_ref[0:seen, lo:mid]
                vals = kv_ref[0:seen, mid:hi]
                for k in range(KA):
                    qk = q_ref[k, :, i * HD : (i + 1) * HD]
                    dok = do_scr[k, :, i * HD : (i + 1) * HD]
                    s = dot(keys, qk, 1, 1)
                    m = jnp.max(s, 0, keepdims=True)
                    p = jnp.exp(s - m)
                    p = p * (1.0 / jnp.sum(p, 0, keepdims=True))
                    t = p * dot(vals, dok, 1, 1)
                    delta = jnp.sum(t, 0, keepdims=True)
                    ds = (t - p * delta).astype(BF)
                    pt_scr[0:seen, k * T : (k + 1) * T] = p.astype(BF)
                    ds_scr[0:seen, k * T : (k + 1) * T] = ds
                    dq_scr[k, :, i * HD : (i + 1) * HD] = (dot(ds, keys, 0, 0) * (HD**-0.5)).astype(BF)
                q_rows = q_ref[:, :, i * HD : (i + 1) * HD].reshape(KA * T, HD)
                do_rows = do_scr[:, :, i * HD : (i + 1) * HD].reshape(KA * T, HD)
                dkv_scr[0:seen, lo:mid] += dot(ds_scr[0:seen, :], q_rows)
                dkv_scr[0:seen, mid:hi] += dot(pt_scr[0:seen, :], do_rows)

    scatter_pairs(ids, [dq_scr[k].astype(F32) for k in range(KA)], a_scr, C)
    dkv = dkv_scr[pl.ds(pl.multiple_of(b * T, T), T), :].astype(BF)
    dx = dot(a_scr[...], wq_ref[...], 1, 1) + dot(dkv, wkv_ref[...], 1, 1)
    dx_ref[...] = dx.astype(dx_ref.dtype)
    gq_scr[...] += dot(xb, a_scr[...], 0, 0)
    gkv_scr[...] += dot(xb, dkv, 0, 0)

    @pl.when(step == nb - 1)
    def _():
        gq_ref[...] = gq_scr[...].astype(BF)
        gkv_ref[...] = gkv_scr[...].astype(BF)
        gout_ref[...] = gout_scr[...].astype(BF)


def attn_backward(x_all, d_all, ids_all, gates, q, kv, mix, wq, wkv, wout, T, hd):
    L, D = x_all.shape
    nb = L // T
    C = hd * HD
    return pl.pallas_call(
        functools.partial(attn_bwd_kernel, nb, hd),
        name="attn_backward",
        grid=(nb,),
        out_shape=(
            jax.ShapeDtypeStruct((L, D), BF),
            jax.ShapeDtypeStruct((L, KA), F32),
            jax.ShapeDtypeStruct((D, EA * C), BF),
            jax.ShapeDtypeStruct((D, 2 * C), BF),
            jax.ShapeDtypeStruct((EA * C, D), BF),
        ),
        in_specs=[
            pl.BlockSpec((T, D), lambda i: (nb - 1 - i, 0)),
            pl.BlockSpec((T, D), lambda i: (nb - 1 - i, 0)),
            pl.BlockSpec((T, KA), lambda i: (nb - 1 - i, 0)),
            pl.BlockSpec((T, KA), lambda i: (nb - 1 - i, 0)),
            pl.BlockSpec((KA, T, C), lambda i: (0, nb - 1 - i, 0)),
            vmem(),
            pl.BlockSpec((KA, T, C), lambda i: (0, nb - 1 - i, 0)),
            vmem(), vmem(), vmem(),
        ],
        out_specs=(
            pl.BlockSpec((T, D), lambda i: (nb - 1 - i, 0)),
            pl.BlockSpec((T, KA), lambda i: (nb - 1 - i, 0)),
            vmem(), vmem(), vmem(),
        ),
        scratch_shapes=[
            pltpu.VMEM((D, EA * C), F32),
            pltpu.VMEM((D, 2 * C), F32),
            pltpu.VMEM((EA * C, D), F32),
            pltpu.VMEM((L, 2 * C), F32),
            pltpu.VMEM((T, EA * C), F32),
            pltpu.VMEM((T, EA * C), BF),
            pltpu.VMEM((KA, T, C), BF),
            pltpu.VMEM((KA, T, C), BF),
            pltpu.VMEM((L, KA * T), BF),
            pltpu.VMEM((L, KA * T), BF),
        ],
    )(x_all, d_all, ids_all, gates, q, kv, mix, wq, wkv, wout)


def rows_of(ref):
    value = ref[...]
    return value.astype(F32).reshape(-1, value.shape[-1]).astype(BF)


def ffn_fwd_kernel(x_ref, w1_ref, w2_ref, out_ref):
    x = rows_of(x_ref)
    FE = w1_ref.shape[-1]
    step = 512
    acc = jnp.zeros((x.shape[0], x.shape[1]), F32)
    for c in range(0, FE, step):
        value, _ = gelu_parts(dot(x, w1_ref[0, :, c : c + step]))
        acc = acc + dot(value.astype(BF), w2_ref[0, c : c + step, :])
    out_ref[...] = acc.reshape(out_ref.shape).astype(BF)


def ffn_bwd_kernel(x_ref, dy_ref, w1_ref, w2_ref, out_ref):
    x = rows_of(x_ref)
    dy = rows_of(dy_ref)
    FE = w1_ref.shape[-1]
    step = 512
    acc = jnp.zeros((x.shape[0], x.shape[1]), F32)
    for c in range(0, FE, step):
        _, slope = gelu_parts(dot(x, w1_ref[0, :, c : c + step]))
        dpre = dot(dy, w2_ref[0, c : c + step, :], 1, 1) * slope
        acc = acc + dot(dpre.astype(BF), w1_ref[0, :, c : c + step], 1, 1)
    out_ref[...] = acc.reshape(out_ref.shape).astype(BF)


def ffn_grad_kernel(x_ref, dy_ref, w1_ref, w2_ref, g1_ref, g2_ref):
    x = rows_of(x_ref)
    dy = rows_of(dy_ref)

    @pl.when(pl.program_id(2) == 0)
    def _():
        g1_ref[...] = jnp.zeros_like(g1_ref)
        g2_ref[...] = jnp.zeros_like(g2_ref)

    value, slope = gelu_parts(dot(x, w1_ref[0]))
    dpre = (dot(dy, w2_ref[0], 1, 1) * slope).astype(BF)
    g1_ref[0] += dot(x, dpre, 0, 0)
    g2_ref[0] += dot(value.astype(BF), dy, 0, 0)


def ffn_specs(W, D, FE):
    return (
        pl.BlockSpec((W, 1, CAP, D), lambda j: (0, j, 0, 0)),
        pl.BlockSpec((1, D, FE), lambda j: (j, 0, 0)),
        pl.BlockSpec((1, FE, D), lambda j: (j, 0, 0)),
    )


def ffn_forward(x, w1, w2):
    W, EL, _, D = x.shape
    rows, one, two = ffn_specs(W, D, w1.shape[-1])
    return pl.pallas_call(
        ffn_fwd_kernel, name="ffn_forward", grid=(EL,),
        out_shape=jax.ShapeDtypeStruct(x.shape, BF),
        in_specs=[rows, one, two], out_specs=rows,
    )(x, w1, w2)


def ffn_backward(x, dy, w1, w2):
    W, EL, _, D = x.shape
    rows, one, two = ffn_specs(W, D, w1.shape[-1])
    return pl.pallas_call(
        ffn_bwd_kernel, name="ffn_backward", grid=(EL,),
        out_shape=jax.ShapeDtypeStruct(x.shape, BF),
        in_specs=[rows, rows, one, two], out_specs=rows,
    )(x, dy, w1, w2)


def ffn_grads(x, dy, w1, w2):
    S, W, EL, _, D = x.shape
    FE = w1.shape[-1]
    ns = max(1, min(S, 768 // (W * CAP)))
    chunk = 512
    rows = pl.BlockSpec((ns, W, 1, CAP, D), lambda j, c, r: (r, 0, j, 0, 0))
    one = pl.BlockSpec((1, D, chunk), lambda j, c, r: (j, 0, c))
    two = pl.BlockSpec((1, chunk, D), lambda j, c, r: (j, c, 0))
    return pl.pallas_call(
        ffn_grad_kernel, name="ffn_grads", grid=(EL, FE // chunk, S // ns),
        out_shape=(jax.ShapeDtypeStruct(w1.shape, F32), jax.ShapeDtypeStruct(w2.shape, F32)),
        in_specs=[rows, rows, one, two], out_specs=(one, two),
    )(x, dy, w1, w2)


def per_device(
    tokens, halted, attn_ids, ffn_ids, norm1, attn_router, attn_kv, attn_query, attn_out,
    norm2, ffn_router, ffn_in, ffn_out, halt_weight, cotangent,
):
    _, T, D = tokens.shape
    S, W = lax.axis_size("seq"), lax.axis_size("wt")
    s = lax.axis_index("seq")
    hd = D // HD // S
    C = hd * HD
    EL = ffn_in.shape[0]
    rows_w = norm1.shape[0]
    slots = EF * CAP

    tokens, halted, attn_ids, ffn_ids = tokens[0], halted[0], attn_ids[0], ffn_ids[0]
    cot = cotangent[0].astype(F32)
    stream = tokens.astype(F32)

    pack = jnp.concatenate(
        [norm1[:, None], norm2[:, None], halt_weight[:, None], attn_router, ffn_router,
         jnp.zeros((rows_w, 128 - C_END), BF)], 1)
    small = lax.all_gather(pack, "wt", axis=0, tiled=True)
    gain1 = small[:, C_N1].astype(F32)[None]
    gain2 = small[:, C_N2].astype(F32)[None]
    halting = small[:, C_HALT].astype(F32)[None]

    wq_mine = lax.dynamic_slice_in_dim(attn_query, s * C, C, 2).transpose(1, 0, 2).reshape(rows_w, EA * C)
    wkv_mine = lax.dynamic_slice_in_dim(attn_kv, s * 2 * C, 2 * C, 1)
    wq = lax.all_gather(wq_mine, "wt", axis=0, tiled=True)
    wkv = lax.all_gather(wkv_mine, "wt", axis=0, tiled=True)
    wo = lax.dynamic_slice_in_dim(attn_out, s * C, C, 2)
    wo = lax.all_gather(wo, "wt", axis=1, tiled=True)
    wout = lax.all_to_all(wo, "seq", split_axis=1, concat_axis=2, tiled=True).reshape(EA * C, D)

    normed1, spread1 = layer_norm(stream)
    attn_in = (normed1 * gain1).astype(BF)
    x_all = lax.all_gather(attn_in, "seq", axis=0, tiled=True)
    ids_all = lax.all_gather(attn_ids, "seq", axis=0, tiled=True)

    part, q, kv, mix, gates_all = attn_forward(x_all, ids_all, small, wq, wkv, wout, T, hd)
    parts = lax.all_to_all(part, "seq", split_axis=0, concat_axis=0, tiled=True).reshape(S, T, D)
    after_attn = stream + jnp.sum(parts.astype(F32), 0)

    normed2, spread2 = layer_norm(after_attn)
    ffn_x = (normed2 * gain2).astype(BF)
    logits = dot(ffn_x, small[:, C_FR:C_END])
    expert = jnp.arange(EF, dtype=jnp.int32)[None]
    hots = [(ffn_ids[:, k : k + 1] == expert).astype(F32) for k in range(KF)]
    picked = jnp.concatenate([jnp.sum(h * logits, -1, keepdims=True) for h in hots], 1)
    gates = jax.nn.softmax(picked, -1)
    before = (jnp.arange(T)[:, None] > jnp.arange(T)[None, :]).astype(BF)
    rank = dot(before, (hots[0] + hots[1]).astype(BF))
    places = [
        ffn_ids[:, k] * CAP + jnp.sum(hots[k] * rank, -1).astype(jnp.int32) for k in range(KF)
    ]
    slot = jnp.arange(slots, dtype=jnp.int32)[None]
    place_hot = [(p[:, None] == slot).astype(BF) for p in places]
    both_hot = place_hot[0] + place_hot[1]

    dispatch = dot(both_hot, ffn_x, 0, 0).astype(BF)
    received = lax.all_to_all(dispatch, "wt", split_axis=0, concat_axis=0, tiled=True)
    received = received.reshape(W, EL, CAP, D)
    slot_out = ffn_forward(received, ffn_in, ffn_out)
    returned = lax.all_to_all(slot_out.reshape(slots, D), "wt", split_axis=0, concat_axis=0, tiled=True)
    expert_rows = [dot(h, returned) for h in place_hot]
    after_ffn = after_attn + gates[:, 0:1] * expert_rows[0] + gates[:, 1:2] * expert_rows[1]
    live = (1 - halted).astype(F32)[:, None]
    halt = jax.nn.sigmoid(jnp.sum(after_ffn * halting, -1, keepdims=True))
    keep = live * (1.0 - halt)
    block_out = (stream + keep * (after_ffn - stream)).astype(BF)

    d_halt = -live * halt * (1.0 - halt) * jnp.sum((after_ffn - stream) * cot, -1, keepdims=True)
    g_halt = jnp.sum(d_halt * after_ffn, 0)
    d_after_ffn = keep * cot + d_halt * halting
    d_slots = sum(
        dot(place_hot[k], (gates[:, k : k + 1] * d_after_ffn).astype(BF), 0, 0) for k in range(KF)
    ).astype(BF)
    d_gates = jnp.concatenate(
        [jnp.sum(r * d_after_ffn, -1, keepdims=True) for r in expert_rows], 1)
    d_received = lax.all_to_all(d_slots, "wt", split_axis=0, concat_axis=0, tiled=True)
    d_received = d_received.reshape(W, EL, CAP, D)
    d_disp = ffn_backward(received, d_received, ffn_in, ffn_out)
    d_disp = lax.all_to_all(d_disp.reshape(slots, D), "wt", split_axis=0, concat_axis=0, tiled=True)

    x_rows = lax.all_gather(received, "seq", axis=0)
    dy_rows = lax.all_gather(d_received, "seq", axis=0)
    g_ffn_in, g_ffn_out = ffn_grads(x_rows, dy_rows, ffn_in, ffn_out)

    d_picked = gates * (d_gates - jnp.sum(gates * d_gates, -1, keepdims=True))
    d_logits = (hots[0] * d_picked[:, 0:1] + hots[1] * d_picked[:, 1:2]).astype(BF)
    g_ffn_router = dot(ffn_x, d_logits, 0, 0)
    d_ffn_x = dot(both_hot, d_disp) + dot(d_logits, small[:, C_FR:C_END], 1, 1)
    g_norm2 = jnp.sum(d_ffn_x * normed2, 0)
    d_after_attn = d_after_ffn + norm_back(d_ffn_x, normed2, spread2, gain2)

    d_all = lax.all_gather(d_after_attn.astype(BF), "seq", axis=0, tiled=True)
    dx, dg, g_q, g_kv, g_out = attn_backward(
        x_all, d_all, ids_all, gates_all, q, kv, mix, wq, wkv, wout, T, hd)
    dx = lax.all_to_all(dx, "seq", split_axis=0, concat_axis=0, tiled=True).reshape(S, T, D)
    dg = lax.psum_scatter(dg, "seq", scatter_dimension=0, tiled=True)
    a_expert = jnp.arange(EA, dtype=jnp.int32)[None]
    a_hots = [(attn_ids[:, k : k + 1] == a_expert).astype(F32) for k in range(KA)]
    a_gates = lax.dynamic_slice_in_dim(gates_all, s * T, T, 0)
    d_pick = a_gates * (dg - jnp.sum(a_gates * dg, -1, keepdims=True))
    d_alogits = sum(a_hots[k] * d_pick[:, k : k + 1] for k in range(KA)).astype(BF)
    g_attn_router = dot(attn_in, d_alogits, 0, 0)
    d_attn_in = jnp.sum(dx.astype(F32), 0) + dot(d_alogits, small[:, C_AR:C_FR], 1, 1)
    g_norm1 = jnp.sum(d_attn_in * normed1, 0)
    g_tokens = (
        (1.0 - keep) * cot + d_after_attn + norm_back(d_attn_in, normed1, spread1, gain1)
    )

    g_pack = jnp.concatenate(
        [g_norm1[:, None], g_norm2[:, None], g_halt[:, None], g_attn_router, g_ffn_router,
         jnp.zeros((D, 128 - C_END), F32)], 1)
    g_pack = lax.psum(lax.psum_scatter(g_pack, "wt", scatter_dimension=0, tiled=True), "seq")
    g_q = lax.psum_scatter(g_q, "wt", scatter_dimension=0, tiled=True)
    g_kv = lax.psum_scatter(g_kv, "wt", scatter_dimension=0, tiled=True)
    g_out = lax.all_to_all(g_out.reshape(EA, C, D), "seq", split_axis=2, concat_axis=1, tiled=True)
    g_out = lax.psum_scatter(g_out, "wt", scatter_dimension=1, tiled=True)
    g_q = lax.all_gather(g_q, "seq", axis=0).reshape(S, rows_w, EA, C)
    g_q = g_q.transpose(2, 1, 0, 3).reshape(EA, rows_w, D).astype(F32)
    g_kv = lax.all_gather(g_kv, "seq", axis=1, tiled=True).astype(F32)
    g_out = lax.all_gather(g_out, "seq", axis=2, tiled=True).astype(F32)

    return (
        block_out[None], g_tokens[None], g_pack[:, C_N1], g_pack[:, C_AR:C_FR], g_kv, g_q, g_out,
        g_pack[:, C_N2], g_pack[:, C_FR:C_END], g_ffn_in, g_ffn_out, g_pack[:, C_HALT],
    )


def solution(mesh):
    tok, exp = P("wt", "seq", None), P(None, "wt", None)
    vec, mat, ffn = P("wt"), P("wt", None), P("wt", None, None)
    return jax.shard_map(
        per_device,
        mesh=mesh,
        in_specs=(tok, P("wt", "seq"), tok, tok, vec, mat, mat, exp, exp, vec, mat, ffn, ffn, vec, tok),
        out_specs=(tok, tok, vec, mat, mat, exp, exp, vec, mat, ffn, ffn, vec),
        check_vma=False,
    )
```

time: 1510 us -> 769 us (0.51)
  waiting for transfers between devices: 792 us -> 299 us
  Pallas kernels: 0 us -> 166 us
  matrix products: 173 us -> 7.94 us
  local copies, waits for them, and re-layouts: 197 us -> 32.6 us
  other arithmetic: 102 us -> 10.8 us
  blocking collectives: 176 us -> 204 us
    psum x1 -> x0, waiting for transfers between devices: 286 us -> none  [per_device(): lax.psum(shards[2].astype(jnp.bfloat16), 'seq').astype(jnp.float32)]
    pallas_call x0 -> x5, Pallas kernels: none -> 166 us  [the longest x1 77.3 us: attn_backward(): pl.pallas_call(functools.partial(attn_bwd_kernel, nb, hd), name='attn_bac...]
    dot_general x51 -> x12, matrix products: 173 us -> 7.94 us  [dot(): lax.dot_general(a, b, (((ca,), (cb,)), ((), ())), preferred_element_type=...]
    reduce_scatter x3 -> x4, waiting for transfers between devices: 242 us -> 115 us  [the longest x1 52.1 us: per_device(): g_out = lax.psum_scatter(g_out, 'wt', scatter_dimension=1, tiled=True)]
    unnamed x11 -> x12, waiting for transfers between devices: 127 us -> 57.2 us
    all_gather x2 -> x6, blocking collectives: 52.9 us -> 112 us  [the longest x1 34.6 us: per_device(): ids_all = lax.all_gather(attn_ids, 'seq', axis=0, tiled=True)]
    convert_element_type x13 -> x3, local copies, waits for them, and re-layouts: 55.4 us -> 5.5 us  [per_device(): g_q = g_q.transpose(2, 1, 0, 3).reshape(EA, rows_w, D).astype(F32)]
    unnamed x242 -> x34, local copies, waits for them, and re-layouts: 55.8 us -> 6.31 us
  transfers between devices with their start and end apart: 15 -> 16, of which waited for: 10 -> 13; matrix products, arithmetic and copies ran while one was open for 13% -> 5% of each run, Pallas kernels for 0% -> 5%
where the time goes in v1:
time: 769 us; the launch traced here: 764 us
  waiting for transfers between devices  299 us (39%)
  blocking collectives  204 us (27%)
  Pallas kernels  166 us (22%)
  local copies, waits for them, and re-layouts  32.6 us (4%)
  starting transfers between devices  28.8 us (4%)
  between operations  14.4 us (2%)
  other arithmetic  10.8 us (1%)
  matrix products  7.94 us (1%)
    pallas_call x1, Pallas kernels, attn_backward(): pl.pallas_call(functools.partial(attn_bwd_kernel, nb, hd), name='attn_bac...  77.3 us
    unnamed x12, waiting for transfers between devices  57.2 us
    reduce_scatter x1, waiting for transfers between devices, per_device(): g_out = lax.psum_scatter(g_out, 'wt', scatter_dimension=1, tiled=True)  52.1 us
    pallas_call x1, Pallas kernels, ffn_grads(): pl.pallas_call(ffn_grad_kernel, name='ffn_grads', grid=(EL, FE // chunk,...  39.4 us
    all_gather x1, blocking collectives, per_device(): ids_all = lax.all_gather(attn_ids, 'seq', axis=0, tiled=True)  34.6 us
    all_gather x1, waiting for transfers between devices, per_device(): dy_rows = lax.all_gather(d_received, 'seq', axis=0)  30 us
    all_to_all x1, blocking collectives, per_device(): lax.all_to_all(g_out.reshape(EA, C, D), 'seq', split_axis=2, concat_axis=...  28.5 us
    reduce_scatter x1, waiting for transfers between devices, per_device(): g_q = lax.psum_scatter(g_q, 'wt', scatter_dimension=0, tiled=True)  27.7 us
  transfers between devices with their start and end apart: 16, of which 13 were waited for; matrix products, arithmetic and copies ran while one was open for 5% of the time, Pallas kernels for 5%

profile of v1, /device:TPU:9, one launch (start us, length us, event | category | flops | bytes accessed | tf_op | source)
XLA Modules:
  0.0 763.9 jit_solution(10142221540590416961)
XLA Ops:
  13.1 22.2 %all_gather.39.small_ref = bf16[512,128]{1,0:T(8,128)(2,1)S(1)} all-gather(bf16[64,128]{1,0:T(8,128)(2,1)S(1)} %concatenate.12), channel_id=1, replica_groups=mesh['seq'=4,'wt'=8] {'wt'}, dimensions={0}, use_global_device_ids=true | all-gather | bytes 147456 | tf_op jit(solution)/shard_map/all_gather | solution.py:387
  39.6 16.6 %all-gather.13.cloned.1.call-done = bf16[12,512,128]{2,1,0:T(8,128)(2,1)} async-done(((bf16[12,64,128]{2,1,0:T(8,128)(2,1)}), bf16[12,512,128]{2,1,0:T(8,128)(2,1)}) %all-gather.13.cloned.1.call-update) | async-done | bytes 1572880 | tf_op jit(solution)/shard_map/all_gather | solution.py:397
  60.0 5.1 all-to-all-start
  65.3 34.6 %all-gather = s32[1,1024,4]{2,1,0:T(8,128)} all-gather(s32[1,256,4]{2,1,0:T(8,128)S(1)} %copy.73), channel_id=2, replica_groups=mesh['seq'=4,'wt'=8] {'seq'}, dimensions={1}, use_global_device_ids=true | all-gather | bytes 20480 | tf_op jit(solution)/shard_map/all_gather | solution.py:403
  100.7 25.4 %all_gather.43.wkv_ref = bf16[512,256]{1,0:T(8,128)(2,1)} all-gather(bf16[64,256]{1,0:T(8,128)(2,1)S(1)} %constant_dynamic-slice_fusion.1), channel_id=1, replica_groups=mesh['seq'=4,'wt'=8] {'wt'}, dimensions={0}, use_global_device_ids=true | all-gather | bytes 294912 | tf_op jit(solution)/shard_map/all_gather | solution.py:395
  128.9 26.7 %attn_forward.1 = (bf16[1024,512]{1,0:T(8,128)(2,1)}, bf16[4,1024,128]{2,1,0:T(8,128)(2,1)}, bf16[1024,256]{1,0:T(8,128)(2,1)}, bf16[4,1024,128]{2,1,0:T(8,128)(2,1)}, f32[1024,4]{1,0:T(8,128)}) custom-call(bf16[1024,512]{1,0:T(8,128)(2,1)} %all-gather.9.cloned.1.call-done.x_ref, s32[1024,4]{1,0:T(8,128)} %bitcast.154, bf16[512,128]{1,0:T(8,128)(2,1)} %copy-done.4, ...), custom_call_target="tpu_custom_call" | custom-call | tf_op jit(solution)/shard_map/attn_forward/pallas_call | solution.py:129
  155.6 9.0 %all-to-all-start.1 = ((bf16[4,256,512]{2,1,0:T(8,128)(2,1)}), bf16[4,256,512]{2,1,0:T(8,128)(2,1)S(1)}, u32[]{:S(2)}, u32[]{:S(2)}) async-start(bf16[4,256,512]{2,1,0:T(8,128)(2,1)} %bitcast.161), calls=%async_computation.1 | async-start | bytes 2097152 | tf_op jit(solution)/shard_map/all_to_all | solution.py:406
  164.6 13.6 %all-to-all-done.1 = bf16[4,256,512]{2,1,0:T(8,128)(2,1)S(1)} async-done(((bf16[4,256,512]{2,1,0:T(8,128)(2,1)}), bf16[4,256,512]{2,1,0:T(8,128)(2,1)S(1)}, u32[]{:S(2)}, u32[]{:S(2)}) %all-to-all-start.1) | async-done | bytes 1048608 | tf_op jit(solution)/shard_map/all_to_all | solution.py:406
  180.3 24.9 %all_to_all.93 = bf16[8,96,512]{2,1,0:T(8,128)(2,1)} all-to-all(bf16[8,96,512]{2,1,0:T(8,128)(2,1)S(1)} %bitcast.162), channel_id=1, replica_groups=mesh['seq'=4,'wt'=8] {'wt'}, dimensions={0} | all-to-all | bytes 1572864 | tf_op jit(solution)/shard_map/all_to_all | solution.py:426
  205.2 10.0 %ffn_forward.1 = bf16[8,4,24,512]{3,2,1,0:T(8,128)(2,1)} custom-call(bf16[8,4,24,512]{3,2,1,0:T(8,128)(2,1)} %bitcast.142, bf16[4,512,2048]{2,1,0:T(8,128)(2,1)} %w1_ref.5, bf16[4,2048,512]{2,1,0:T(8,128)(2,1)} %w2_ref.5), custom_call_target="tpu_custom_call" | custom-call | tf_op jit(solution)/shard_map/ffn_forward/pallas_call | solution.py:335
  215.3 5.3 all-to-all-start.3
  220.6 16.5 %all-to-all-done.3 = bf16[8,96,512]{2,1,0:T(8,128)(2,1)S(1)} async-done(((bf16[8,96,512]{2,1,0:T(8,128)(2,1)}), bf16[8,96,512]{2,1,0:T(8,128)(2,1)S(1)}, u32[]{:S(2)}, u32[]{:S(2)}) %all-to-all-start.3) | async-done | bytes 786464 | tf_op jit(solution)/shard_map/all_to_all | solution.py:429
  240.1 25.6 %all_to_all.94 = bf16[8,96,512]{2,1,0:T(8,128)(2,1)} all-to-all(bf16[8,96,512]{2,1,0:T(8,128)(2,1)S(1)} %bitcast.158), channel_id=1, replica_groups=mesh['seq'=4,'wt'=8] {'wt'}, dimensions={0} | all-to-all | bytes 1572864 | tf_op jit(solution)/shard_map/all_to_all | solution.py:445
  265.7 12.5 %ffn_backward.1 = bf16[8,4,24,512]{3,2,1,0:T(8,128)(2,1)} custom-call(bf16[8,4,24,512]{3,2,1,0:T(8,128)(2,1)} %bitcast.143, bf16[8,4,24,512]{3,2,1,0:T(8,128)(2,1)} %bitcast.148, bf16[4,512,2048]{2,1,0:T(8,128)(2,1)} %w1_ref.5, bf16[4,2048,512]{2,1,0:T(8,128)(2,1)} %w2_ref.5), custom_call_target="tpu_custom_call" | custom-call | tf_op jit(solution)/shard_map/ffn_backward/pallas_call | solution.py:345
  278.1 5.2 all-to-all-start.5
  284.7 14.8 %all-to-all-done.5 = bf16[8,96,512]{2,1,0:T(8,128)(2,1)} async-done(((bf16[8,96,512]{2,1,0:T(8,128)(2,1)}), bf16[8,96,512]{2,1,0:T(8,128)(2,1)}, u32[]{:S(2)}, u32[]{:S(2)}) %all-to-all-start.5) | async-done | bytes 786464 | tf_op jit(solution)/shard_map/all_to_all | solution.py:448
  302.6 19.5 %all-gather.15.cloned.1.call-done.d_ref = bf16[1024,512]{1,0:T(8,128)(2,1)} async-done(((bf16[256,512]{1,0:T(8,128)(2,1)}), bf16[1024,512]{1,0:T(8,128)(2,1)}) %all-gather.15.cloned.1.call-update) | async-done | bytes 1048592 | tf_op jit(solution)/shard_map/all_gather | solution.py:461
  322.0 77.3 %attn_backward.1 = (bf16[1024,512]{1,0:T(8,128)(2,1)}, f32[1024,4]{1,0:T(8,128)}, bf16[512,1536]{1,0:T(8,128)(2,1)}, bf16[512,256]{1,0:T(8,128)(2,1)}, bf16[1536,512]{1,0:T(8,128)(2,1)}) custom-call(bf16[1024,512]{1,0:T(8,128)(2,1)} %all-gather.9.cloned.1.call-done.x_ref, bf16[1024,512]{1,0:T(8,128)(2,1)} %all-gather.15.cloned.1.call-done.d_ref, ...), custom_call_target="tpu_custom_call" | custom-call | tf_op jit(solution)/shard_map/attn_backward/pallas_call | solution.py:239
  403.9 16.9 %reduce-scatter.8.cloned.1.call-done = f32[256,4]{1,0:T(8,128)} async-done(((f32[1024,4]{1,0:T(8,128)}), f32[256,4]{1,0:T(8,128)}) %reduce-scatter.8.cloned.1.call-update) | async-done | bytes 4112 | tf_op jit(solution)/shard_map/reduce_scatter | solution.py:465
  432.1 28.5 %all_to_all.95 = bf16[12,128,512]{1,0,2:T(8,128)(2,1)} all-to-all(bf16[12,128,512]{1,0,2:T(8,128)(2,1)S(1)} %copy.78), channel_id=1, replica_groups=mesh['seq'=4,'wt'=8] {'seq'}, dimensions={2} | all-to-all | bytes 3145728 | tf_op jit(solution)/shard_map/all_to_all | solution.py:484
  460.6 4.3 copy.79
  465.0 18.4 %reduce-scatter.10.cloned.1.call-done = bf16[64,256]{1,0:T(8,128)(2,1)} async-done(((bf16[512,256]{1,0:T(8,128)(2,1)}), bf16[64,256]{1,0:T(8,128)(2,1)}) %reduce-scatter.10.cloned.1.call-update) | async-done | bytes 32784 | tf_op jit(solution)/shard_map/reduce_scatter | solution.py:483
  483.5 8.2 %all_gather.46 = bf16[64,1024]{1,0:T(8,128)(2,1)S(1)} all-gather(bf16[64,256]{1,0:T(8,128)(2,1)} %reduce-scatter.10.cloned.1.call-done), channel_id=1, replica_groups=mesh['seq'=4,'wt'=8] {'seq'}, dimensions={1}, use_global_device_ids=true | all-gather | bytes 163840 | tf_op jit(solution)/shard_map/all_gather | solution.py:488
  493.4 54.7 %reduce-scatter.16.cloned.1.call-done = f32[64,128]{1,0:T(8,128)} async-done(((f32[512,128]{1,0:T(8,128)}), f32[64,128]{1,0:T(8,128)}) %reduce-scatter.16.cloned.1.call-update) | async-done | bytes 32784
  549.0 13.3 %psum.7 = f32[64,128]{0,1:T(8,128)S(1)} all-reduce(f32[64,128]{0,1:T(8,128)S(1)} %copy.81), channel_id=1, replica_groups=mesh['seq'=4,'wt'=8] {'seq'}, use_global_device_ids=true, to_apply=%region_26.0 | all-reduce | flops 8192 | bytes 65536 | tf_op jit(solution)/shard_map/psum | solution.py:481
  564.0 16.0 %all-gather.17.cloned.1.call-done.x_ref = bf16[4,8,4,24,512]{4,3,2,1,0:T(8,128)(2,1)} async-done(((bf16[1,8,4,24,512]{4,3,2,1,0:T(8,128)(2,1)}), bf16[4,8,4,24,512]{4,3,2,1,0:T(8,128)(2,1)}) %all-gather.17.cloned.1.call-update) | async-done | bytes 3145744 | tf_op jit(solution)/shard_map/all_gather | solution.py:450
  580.0 30.0 %all-gather.19.cloned.1.call-done.dy_ref = bf16[4,8,4,24,512]{4,3,2,1,0:T(8,128)(2,1)} async-done(((bf16[1,8,4,24,512]{4,3,2,1,0:T(8,128)(2,1)}), bf16[4,8,4,24,512]{4,3,2,1,0:T(8,128)(2,1)}) %all-gather.19.cloned.1.call-update) | async-done | bytes 3145744 | tf_op jit(solution)/shard_map/all_gather | solution.py:451
  610.0 39.4 %ffn_grads.1 = (f32[4,512,2048]{2,1,0:T(8,128)}, f32[4,2048,512]{2,1,0:T(8,128)}) custom-call(bf16[4,8,4,24,512]{4,3,2,1,0:T(8,128)(2,1)} %all-gather.17.cloned.1.call-done.x_ref, bf16[4,8,4,24,512]{4,3,2,1,0:T(8,128)(2,1)} %all-gather.19.cloned.1.call-done.dy_ref, bf16[4,512,2048]{2,1,0:T(8,128)(2,1)} %w1_ref.5, bf16[4,2048,512]{2,1,0:T(8,128)(2,1)} %w2_ref.5), custom_call_target="tpu_custom_call" | custom-call | tf_op jit(solution)/shard_map/ffn_grads/pallas_call | solution.py:360
  649.4 27.7 %reduce-scatter.12.cloned.1.call-done = bf16[64,1536]{1,0:T(8,128)(2,1)} async-done(((bf16[512,1536]{1,0:T(8,128)(2,1)}), bf16[64,1536]{1,0:T(8,128)(2,1)}) %reduce-scatter.12.cloned.1.call-update) | async-done | bytes 196624 | tf_op jit(solution)/shard_map/reduce_scatter | solution.py:482
  677.0 10.6 %all-gather.1 = bf16[256,1536]{1,0:T(8,128)(2,1)S(1)} all-gather(bf16[64,1536]{1,0:T(8,128)(2,1)} %reduce-scatter.12.cloned.1.call-done), channel_id=3, replica_groups=mesh['seq'=4,'wt'=8] {'seq'}, dimensions={0}, use_global_device_ids=true | all-gather | bytes 983040 | tf_op jit(solution)/shard_map/all_gather | solution.py:486
  693.1 52.1 %reduce-scatter.14.cloned.1.call-done = bf16[12,64,128]{2,1,0:T(8,128)(2,1)} async-done(((bf16[12,512,128]{2,1,0:T(8,128)(2,1)}), bf16[12,64,128]{2,1,0:T(8,128)(2,1)}) %reduce-scatter.14.cloned.1.call-update) | async-done | bytes 196624 | tf_op jit(solution)/shard_map/reduce_scatter | solution.py:485
  745.2 10.6 %all_gather.49 = bf16[12,64,512]{2,1,0:T(8,128)(2,1)S(1)} all-gather(bf16[12,64,128]{2,1,0:T(8,128)(2,1)} %reduce-scatter.14.cloned.1.call-done), channel_id=1, replica_groups=mesh['seq'=4,'wt'=8] {'seq'}, dimensions={2}, use_global_device_ids=true | all-gather | bytes 983040 | tf_op jit(solution)/shard_map/all_gather | solution.py:489
  (130 shorter events, 54.0 us)
Async XLA Ops:
  7.2 1.1 copy-start
  7.2 29.6 %copy-start.2 = (bf16[1,256,512]{2,1,0:T(8,128)(2,1)S(1)}, bf16[1,256,512]{2,1,0:T(8,128)(2,1)}, u32[]{:S(2)}) copy-start(bf16[1,256,512]{2,1,0:T(8,128)(2,1)} %param.15) | copy-start | bytes 786436
  7.2 49.0 %all-gather.13.cloned.1.call-start = ((), (), s32[]{:S(2)}) async-start(), calls=%async_computation.15 | async-start | bytes 1769472 | tf_op jit(solution)/shard_map/all_gather | solution.py:397
  9.1 119.6 %all-gather.9.cloned.1.call-start = ((), (), s32[]{:S(2)}) async-start(), calls=%async_computation.13 | async-start | bytes 1310720 | tf_op jit(solution)/shard_map/all_gather | solution.py:402
  35.3 24.7 %copy-start.4 = (bf16[512,128]{1,0:T(8,128)(2,1)}, bf16[512,128]{1,0:T(8,128)(2,1)S(1)}, u32[]{:S(2)}) copy-start(bf16[512,128]{1,0:T(8,128)(2,1)S(1)} %all_gather.39.small_ref) | copy-start | bytes 393220
  37.9 91.0 %all-gather.11.cloned.1.call-start = ((), (), s32[]{:S(2)}) async-start(), calls=%async_computation.14 | async-start | bytes 1769472 | tf_op jit(solution)/shard_map/all_gather | solution.py:394
  60.0 5.1 copy-start.11
  60.0 66.0 %all-to-all-start = ((bf16[12,512,128]{2,0,1:T(8,128)(2,1)}), bf16[12,512,128]{2,0,1:T(8,128)(2,1)S(1)}, u32[]{:S(2)}, u32[]{:S(2)}) async-start(bf16[12,512,128]{2,0,1:T(8,128)(2,1)} %copy.75), calls=%async_computation | async-start | bytes 4194304 | tf_op jit(solution)/shard_map/all_to_all | solution.py:398
  155.6 9.0 %copy-start.12 = (s32[1,256,2]{1,2,0:T(2,128)S(1)}, s32[1,256,2]{1,2,0:T(2,128)}, u32[]{:S(2)}) copy-start(s32[1,256,2]{1,2,0:T(2,128)} %param.18) | copy-start | bytes 6148
  155.6 22.6 %all-to-all-start.1 = ((bf16[4,256,512]{2,1,0:T(8,128)(2,1)}), bf16[4,256,512]{2,1,0:T(8,128)(2,1)S(1)}, u32[]{:S(2)}, u32[]{:S(2)}) async-start(bf16[4,256,512]{2,1,0:T(8,128)(2,1)} %bitcast.161), calls=%async_computation.1 | async-start | bytes 2097152 | tf_op jit(solution)/shard_map/all_to_all | solution.py:406
  178.4 0.9 copy-start.5
  215.3 5.3 copy-start.13
  215.3 22.3 %copy-start.3 = (bf16[1,256,512]{2,1,0:T(8,128)(2,1)S(1)}, bf16[1,256,512]{2,1,0:T(8,128)(2,1)}, u32[]{:S(2)}) copy-start(bf16[1,256,512]{2,1,0:T(8,128)(2,1)} %param.29) | copy-start | bytes 786436
  215.3 21.9 %all-to-all-start.3 = ((bf16[8,96,512]{2,1,0:T(8,128)(2,1)}), bf16[8,96,512]{2,1,0:T(8,128)(2,1)S(1)}, u32[]{:S(2)}, u32[]{:S(2)}) async-start(bf16[8,96,512]{2,1,0:T(8,128)(2,1)} %bitcast.157), calls=%async_computation.3 | async-start | bytes 1572864 | tf_op jit(solution)/shard_map/all_to_all | solution.py:429
  278.1 5.2 copy-start.7
  278.1 21.4 %all-to-all-start.5 = ((bf16[8,96,512]{2,1,0:T(8,128)(2,1)}), bf16[8,96,512]{2,1,0:T(8,128)(2,1)}, u32[]{:S(2)}, u32[]{:S(2)}) async-start(bf16[8,96,512]{2,1,0:T(8,128)(2,1)} %bitcast.156), calls=%async_computation.5 | async-start | bytes 1572864 | tf_op jit(solution)/shard_map/all_to_all | solution.py:448
  283.3 38.7 %all-gather.15.cloned.1.call-start = ((), (), s32[]{:S(2)}) async-start(), calls=%async_computation.16 | async-start | bytes 1310720 | tf_op jit(solution)/shard_map/all_gather | solution.py:461
  302.5 118.3 %reduce-scatter.8.cloned.1.call-start = ((), (), s32[]{:S(2)}) async-start(), calls=%async_computation.17 | async-start | bytes 655360 | tf_op jit(solution)/shard_map/reduce_scatter | solution.py:465
  399.3 21.5 %copy-start.8 = (f32[1024,4]{1,0:T(8,128)S(1)}, f32[1024,4]{1,0:T(8,128)}, u32[]{:S(2)}) copy-start(f32[1024,4]{1,0:T(8,128)} %get-tuple-element.25.gate_ref) | copy-start | bytes 49156
  399.3 23.9 %copy-start.9 = (bf16[256,512]{1,0:T(8,128)(2,1)S(1)}, bf16[256,512]{1,0:T(8,128)(2,1)}, u32[]{:S(2)}) copy-start(bf16[256,512]{1,0:T(8,128)(2,1)} %fusion.15) | copy-start | bytes 786436
  399.3 24.4 %all-to-all-start.6 = ((bf16[4,256,512]{2,1,0:T(8,128)(2,1)}), bf16[4,256,512]{2,1,0:T(8,128)(2,1)S(1)}, u32[]{:S(2)}, u32[]{:S(2)}) async-start(bf16[4,256,512]{2,1,0:T(8,128)(2,1)} %bitcast.160), calls=%async_computation.6 | async-start | bytes 2097152 | tf_op jit(solution)/shard_map/all_to_all | solution.py:464
  403.3 80.2 %reduce-scatter.10.cloned.1.call-start = ((), (), s32[]{:S(2)}) async-start(), calls=%async_computation.18 | async-start | bytes 294912 | tf_op jit(solution)/shard_map/reduce_scatter | solution.py:483
  403.8 144.3 %reduce-scatter.16.cloned.1.call-start = ((), (), s32[]{:S(2)}) async-start(), calls=%async_computation.23 | async-start | bytes 294912
  426.7 153.3 %all-gather.17.cloned.1.call-start = ((), (), s32[]{:S(2)}) async-start(), calls=%async_computation.21 | async-start | bytes 3932160 | tf_op jit(solution)/shard_map/all_gather | solution.py:450
  427.4 182.6 %all-gather.19.cloned.1.call-start = ((), (), s32[]{:S(2)}) async-start(), calls=%async_computation.22 | async-start | bytes 3932160 | tf_op jit(solution)/shard_map/all_gather | solution.py:451
  428.1 248.9 %reduce-scatter.12.cloned.1.call-start = ((), (), s32[]{:S(2)}) async-start(), calls=%async_computation.19 | async-start | bytes 1769472 | tf_op jit(solution)/shard_map/reduce_scatter | solution.py:482
  428.7 316.5 %reduce-scatter.14.cloned.1.call-start = ((), (), s32[]{:S(2)}) async-start(), calls=%async_computation.20 | async-start | bytes 1769472 | tf_op jit(solution)/shard_map/reduce_scatter | solution.py:485
  465.0 27.4 %copy-start.6 = (f32[256,512]{1,0:T(8,128)S(1)}, f32[256,512]{1,0:T(8,128)}, u32[]{:S(2)}) copy-start(f32[256,512]{1,0:T(8,128)} %get-tuple-element.63) | copy-start | bytes 1572868
  465.0 27.4 %copy-start.10 = (f32[256,512]{1,0:T(8,128)S(1)}, f32[256,512]{1,0:T(8,128)}, u32[]{:S(2)}) copy-start(f32[256,512]{1,0:T(8,128)} %get-tuple-element.86) | copy-start | bytes 1572868
  690.2 66.9 %copy-start.1 = (bf16[12,64,512]{2,1,0:T(8,128)(2,1)S(1)}, bf16[12,64,512]{2,1,0:T(8,128)(2,1)}, u32[]{:S(2)}) copy-start(bf16[12,64,512]{2,1,0:T(8,128)(2,1)} %param.23) | copy-start | bytes 2359300
Sparse Core Ops, SparseCore 0:
  10.8 45.3 all-gather.12
  58.4 21.7 all-gather.8
  82.9 45.9 all-gather.10
  302.6 19.3 all-gather.14
  399.5 21.3 reduce-scatter.7
  424.4 59.0 reduce-scatter.9
  487.7 60.3 reduce-scatter.15
  549.8 30.1 all-gather.16
  581.6 28.3 all-gather.18
  614.2 62.7 reduce-scatter.11
  680.5 64.6 reduce-scatter.13
